TPU v7x, 256 devices: a whole 4x4x8 slice. The times are simulated.
256 devices in a mesh: walker: 64 (over x_hi, y, z), freq: 4 (over x_lo, core).
Axes of the slice: x: 4 (x_hi: 2, x_lo: 2; x = x_hi * 2 + x_lo), y: 4, z: 8, core: 2. Of those that a mesh axis runs over, the one named last changes fastest.
Arguments:
- green_up_blocks: bfloat16 [64, 1, 4, 4288], P('walker', None, 'freq'), may hold values from -6 to 6
- green_down_blocks: bfloat16 [64, 1, 4, 4288], P('walker', None, 'freq'), may hold values from -6 to 6
- nu_index: int32 [4], P('freq'), may hold values from 0 to 3, each once
- q_index: int32 [4], P('freq'), may hold values from 0 to 63
- source: float32 [4, 4096], P('freq', 'walker'), may hold values from -6 to 6
Outputs:
- g4: float32 [4, 4096, 4096], P('freq', 'walker')
- response: float32 [4, 4096], P('freq', 'walker')
All inputs are finite; a program needn't handle non-finite values.
Results may differ from a plain program's by a relative error of at most 0.004.
Values may be sent and summed in bfloat16 or wider, within the bound.
No kernel may reach another device: no remote copies, remote signals or barrier semaphores. Data moves between devices by JAX's collectives and lax.ppermute only.
A program may use at most 64 MiB of HBM per device.

v0:
```python
import math

import jax
import jax.numpy as jnp
from jax import lax
from jax.sharding import PartitionSpec as P

SIDE = 8
CLUSTER_MOMENTUM = 64
W = 64
NU = 4
ITERS = 2


def cluster_sum(sites, shift):
    return (sites // SIDE + shift // SIDE) % SIDE * SIDE + (sites % SIDE + shift % SIDE) % SIDE


def products(block, sites, shift, offset):
    moved = cluster_sum(sites, shift)
    base = jnp.take(block, sites, axis=1)[:, :, :W].astype(jnp.float32)
    other = lax.dynamic_slice_in_dim(jnp.take(block, moved, axis=1), offset, W, 2).astype(
        jnp.float32
    )
    return (base * other).astype(jnp.bfloat16).reshape(block.shape[0], sites.shape[0] * W)


def stacked(block, sites, nu_index, q_index):
    return jnp.stack([products(block, sites, q_index[0], nu_index[0])])


def accumulate(left, right):
    return jnp.einsum("nrk,nrc->nkc", left, right, preferred_element_type=jnp.float32)


def shards(green_up_blocks, green_down_blocks, nu_index, q_index, source):
    up_all, down_all = (
        lax.all_gather(green_up_blocks, "freq", axis=2, tiled=True),
        lax.all_gather(green_down_blocks, "freq", axis=2, tiled=True),
    )
    extent = W + NU - 1
    rows_one = up_all.shape[1] * up_all.shape[2]
    walkers = lax.axis_size("walker")
    per_dev = CLUSTER_MOMENTUM // walkers
    owned = lax.axis_index("walker") * per_dev + jnp.arange(per_dev, dtype=jnp.int32)
    every = jnp.arange(CLUSTER_MOMENTUM, dtype=jnp.int32)

    def blocks(piece):
        return piece.reshape(-1, CLUSTER_MOMENTUM, extent)

    left = stacked(
        blocks(lax.all_gather(up_all, "walker", axis=0, tiled=True)), owned, nu_index, q_index
    )
    right = stacked(
        blocks(lax.all_gather(down_all, "walker", axis=0, tiled=True)), every, nu_index, q_index
    )
    summed = accumulate(left, right)
    kernel = summed * (1.0 / math.sqrt(walkers * rows_one))
    scale = 1.0 / (2.0 * math.sqrt(CLUSTER_MOMENTUM * W))
    start_vec = source.T
    current = start_vec
    for step in range(ITERS):

        def term(begin, sample_count, current=current):
            return jnp.einsum("kn,nkc->cn", current, kernel, precision=lax.Precision.HIGHEST)

        current = start_vec + scale * lax.psum_scatter(
            term(jnp.int32(0), lax.axis_size("walker") * (per_dev * W)),
            "walker",
            scatter_dimension=0,
            tiled=True,
        )
    return (kernel, current.T)


def solution(mesh):
    in_specs = (
        P("walker", None, "freq", None),
        P("walker", None, "freq", None),
        P("freq"),
        P("freq"),
        P("freq", "walker"),
    )
    out_specs = (P("freq", "walker", None), P("freq", "walker"))
    return jax.shard_map(shards, mesh=mesh, in_specs=in_specs, out_specs=out_specs, check_vma=False)
```

profile of v0, /device:TPU:2, one launch (start us, length us, event | category | flops | bytes accessed | tf_op | source)
XLA Modules:
  0.0 1031.1 jit_solution(13348956791322953057)
XLA Ops:
  7.2 0.0 all-gather.3.cloned.1.call-start
  7.2 5.7 all_gather.12
  13.0 0.6 copy.18
  13.6 0.0 all-gather.3.cloned.1.call-update
  13.6 0.0 all-gather.5.cloned.1.call-start
  13.6 5.7 all_gather.14
  19.4 0.6 copy.22
  20.0 0.0 all-gather.5.cloned.1.call-update
  20.0 0.0 reduce-scatter.7.cloned.1.call-start
  21.5 112.9 %all-gather.3.cloned.1.call-done = bf16[64,1,4,4288]{3,2,1,0:T(4,128)(2,1)} async-done(((bf16[1,1,4,4288]{3,2,1,0:T(4,128)(2,1)}), bf16[64,1,4,4288]{3,2,1,0:T(4,128)(2,1)}) %all-gather.3.cloned.1.call-update) | async-done | bytes 2195472 | tf_op jit(solution)/shard_map/all_gather | solution.py:52
  134.4 15.4 %reshape.59 = bf16[256,64,67]{2,1,0:T(8,128)(2,1)} reshape(bf16[64,1,4,4288]{3,2,1,0:T(4,128)(2,1)} %all-gather.3.cloned.1.call-done) | data formatting | bytes 4390912 | tf_op jit(solution)/shard_map/reshape | solution.py:49
  149.9 1.5 constant_dynamic-slice_fusion.1
  151.4 0.2 constant_dynamic-slice_fusion.2
  151.6 0.1 copy.32
  151.7 0.1 copy.31
  151.8 102.3 %all-gather.5.cloned.1.call-done = bf16[64,1,4,4288]{3,2,1,0:T(4,128)(2,1)} async-done(((bf16[1,1,4,4288]{3,2,1,0:T(4,128)(2,1)}), bf16[64,1,4,4288]{3,2,1,0:T(4,128)(2,1)}) %all-gather.5.cloned.1.call-update) | async-done | bytes 2195472 | tf_op jit(solution)/shard_map/all_gather | solution.py:55
  254.1 15.4 %reshape.61 = bf16[256,64,67]{2,1,0:T(8,128)(2,1)} reshape(bf16[64,1,4,4288]{3,2,1,0:T(4,128)(2,1)} %all-gather.5.cloned.1.call-done) | data formatting | bytes 4390912 | tf_op jit(solution)/shard_map/reshape | solution.py:49
  269.5 6.7 copy.23
  276.2 2.1 gather_fusion.1
  278.3 2.1 gather_fusion
  280.4 2.9 select_bitcast_fusion
  283.3 1.3 multiply_convert_fusion
  284.6 0.0 copy-start.1
  284.6 0.8 convolution_multiply_fusion
  285.3 0.0 copy-done.1
  285.3 0.0 copy-start
  285.3 4.8 convolution_bitcast_fusion.1
  290.1 0.0 reduce-scatter.7.cloned.1.call-update
  290.1 0.0 reduce-scatter.9.cloned.1.call-start
  290.2 365.8 %reduce-scatter.7.cloned.1.call-done = f32[64,1]{1,0:T(8,128)} async-done(((f32[4096,1]{1,0:T(8,128)}), f32[64,1]{1,0:T(8,128)}) %reduce-scatter.7.cloned.1.call-update) | async-done | bytes 272
  656.0 0.8 copy.26
  656.9 0.0 copy-done
  656.9 4.8 convolution_bitcast_fusion
  661.6 0.0 reduce-scatter.9.cloned.1.call-update
  661.7 361.6 %reduce-scatter.9.cloned.1.call-done = f32[64,1]{1,0:T(8,128)} async-done(((f32[4096,1]{1,0:T(8,128)}), f32[64,1]{1,0:T(8,128)}) %reduce-scatter.9.cloned.1.call-update) | async-done | bytes 272
  1023.2 0.8 copy.28
  1024.1 0.5 fusion.14
  (5 shorter events, 0.0 us)
Async XLA Ops:
  7.2 127.3 %all-gather.3.cloned.1.call-start = ((), (), s32[]{:S(2)}) async-start(), calls=%async_computation.2 | async-start | bytes 2263040 | tf_op jit(solution)/shard_map/all_gather | solution.py:52
  13.6 240.5 %all-gather.5.cloned.1.call-start = ((), (), s32[]{:S(2)}) async-start(), calls=%async_computation.3 | async-start | bytes 2263040 | tf_op jit(solution)/shard_map/all_gather | solution.py:55
  20.0 636.0 %reduce-scatter.7.cloned.1.call-start = ((), (), s32[]{:S(2)}) async-start(), calls=%async_computation.4 | async-start | bytes 2129920
  284.6 0.8 copy-start.1
  285.3 371.5 %copy-start = (f32[64,4096]{1,0:T(8,128)}, f32[64,4096]{1,0:T(8,128)S(1)}, u32[]{:S(2)}) copy-start(f32[64,4096]{1,0:T(8,128)S(1)} %convolution_multiply_fusion) | copy-start | bytes 3145732
  290.1 733.1 %reduce-scatter.9.cloned.1.call-start = ((), (), s32[]{:S(2)}) async-start(), calls=%async_computation.5 | async-start | bytes 2129920
Sparse Core Ops, SparseCore 0:
  13.7 120.6 all-gather.2
  138.6 115.4 all-gather.4
  290.3 365.7 reduce-scatter.6
  661.8 361.4 reduce-scatter.8
where the time goes:
time: 1030 us
  waiting for transfers between devices  943 us (92%)
  local copies, waits for them, and re-layouts  46.5 us (5%)
  between operations  15.3 us (1%)
  blocking collectives  11.5 us (1%)
  matrix products  10.3 us (1%)
    unnamed x6, waiting for transfers between devices  727 us
    all_gather x1, waiting for transfers between devices, shards(): lax.all_gather(up_all, 'walker', axis=0, tiled=True)  113 us
    all_gather x1, waiting for transfers between devices, shards(): lax.all_gather(down_all, 'walker', axis=0, tiled=True)  102 us
    reshape x3, local copies, waits for them, and re-layouts, blocks(): return piece.reshape(-1, CLUSTER_MOMENTUM, extent)  37.5 us
  transfers between devices with their start and end apart: 4, of which 4 were waited for; matrix products, arithmetic and copies ran while one was open for 2% of the time, Pallas kernels for 0%

commit v1 on v0

v1 whole, which is shorter than its diff:
```python
import math

import jax
import jax.numpy as jnp
from jax import lax
from jax.experimental import pallas as pl
from jax.experimental.pallas import tpu as pltpu
from jax.sharding import Mesh, PartitionSpec as P

SIDE = 8
CLUSTER_MOMENTUM = 64
W = 64
NU = 4
ITERS = 2
EXTENT = W + NU - 1
SITES = CLUSTER_MOMENTUM * W
RUN = SIDE * EXTENT
GROUP = 640
SPIN = SIDE * GROUP
OUT = SIDE * W
CHIPS = ("xh", "y", "z", "xl")
LANES = 128
PLANE = GROUP // LANES


def selector(turn, offset):
    row = lax.broadcasted_iota(jnp.int32, (GROUP, OUT), 0)
    col = lax.broadcasted_iota(jnp.int32, (GROUP, OUT), 1)
    want = ((col // W + turn) & (SIDE - 1)) * EXTENT + (col & (W - 1)) + offset
    return jnp.where(row == want, 1.0, 0.0).astype(jnp.bfloat16)


def kernel(where_ref, mine_ref, theirs_ref, s_ref, own_ref, g4_ref, out_ref, up_ref, down_ref, t_ref):
    jump, turn, offset, site = where_ref[0], where_ref[1], where_ref[2], where_ref[3]
    half = mine_ref.shape[0]
    rows = 2 * half
    here = selector(0, 0)
    there = selector(turn, offset)
    f32 = jnp.float32

    def load(group, spin):
        cols = pl.ds(pl.multiple_of(group * GROUP + spin * SPIN, LANES), GROUP)
        return [mine_ref[:, cols], theirs_ref[:, cols]]

    def step(a, carry):
        moved = (a + jump) & (SIDE - 1)
        lhs = jnp.concatenate(load(a, 0) + load(a, 1), axis=0)
        rhs = jnp.concatenate(load(moved, 0) + load(moved, 1), axis=0)
        base = jnp.dot(lhs, here, preferred_element_type=f32)
        other = jnp.dot(rhs, there, preferred_element_type=f32)
        prod = (base * other).astype(jnp.bfloat16)
        cols = pl.ds(pl.multiple_of(a * OUT, LANES), OUT)
        up_ref[:, cols] = prod[:rows]
        down_ref[:, cols] = prod[rows:]
        return carry

    lax.fori_loop(0, SIDE, step, 0)
    norm = 1.0 / math.sqrt(rows)
    scale = norm / (2.0 * math.sqrt(SITES))
    pair = pl.ds(pl.multiple_of((site // 2) * LANES, LANES), LANES)
    odd = site & 1
    t_ref[...] = up_ref[:, pair].astype(f32).T
    left = t_ref[pl.ds(pl.multiple_of(odd * W, W), W), :].astype(jnp.bfloat16)
    nt = (((1,), (1,)), ((), ()))
    g4_ref[0] = jnp.dot(left, down_ref[...], preferred_element_type=f32) * norm
    s = s_ref[...]
    hi = s.astype(jnp.bfloat16)
    rest = s - hi.astype(f32)
    mid = rest.astype(jnp.bfloat16)
    lo = (rest - mid.astype(f32)).astype(jnp.bfloat16)
    up = up_ref[...]
    t0 = sum(lax.dot_general(p, up, nt, preferred_element_type=f32) for p in (hi, mid, lo))
    gram = lax.dot_general(down_ref[...], up, nt, preferred_element_type=f32)
    t0_col = t0.T[:, :1]
    t_row = t0[:1]
    for _ in range(ITERS - 1):
        t_row = t0[:1] + scale * jnp.sum(gram * t0_col, axis=0, keepdims=True)
    t_col = jnp.broadcast_to(t_row, t0.shape).T[:, :1]
    add = jnp.sum(down_ref[:, pair].astype(f32) * t_col, axis=0, keepdims=True)
    add = jnp.where(odd == 1, add[:, W:], add[:, :W])
    out_ref[...] = own_ref[...] + scale * add


def pieces(values):
    first = lax.reduce_precision(values, 8, 7)
    rest = values - first
    second = lax.reduce_precision(rest, 8, 7)
    third = lax.reduce_precision(rest - second, 8, 7)
    return [p.astype(jnp.bfloat16) for p in (first, second, third)]


def spread(block, extra):
    room = GROUP - RUN
    tail = jnp.zeros((SIDE, room), jnp.bfloat16)
    if extra is not None:
        tail = jnp.pad(jnp.concatenate(extra, 0), ((0, SIDE - len(extra)), (0, room - W)))
    return jnp.concatenate([block.reshape(SIDE, RUN), tail], 1).reshape(SPIN // LANES, LANES)


def shards(green_up_blocks, green_down_blocks, nu_index, q_index, source):
    parts = pieces(source)
    block = jnp.concatenate([spread(green_up_blocks, parts), spread(green_down_blocks, None)], 0)
    chips = lax.axis_size(CHIPS)
    depth = block.shape[0]
    mine = lax.all_to_all(
        jnp.broadcast_to(block[None], (chips,) + block.shape), CHIPS, 0, 0, tiled=True
    )
    planes = mine.reshape(chips // 2, 2, depth, LANES)
    planes = lax.dynamic_index_in_dim(planes, lax.axis_index("xl"), 1, False)
    at = RUN - (PLANE - 1) * LANES
    s = sum(
        planes[:, (g + 1) * PLANE - 1, at : at + W].astype(jnp.float32) for g in (2, 1, 0)
    ).reshape(1, SITES)
    mine = mine.reshape(chips, depth * LANES)
    theirs = lax.ppermute(mine, "c", [(0, 1), (1, 0)])
    site = lax.axis_index(("xh", "y", "z"))
    where = jnp.stack([q_index[0] // SIDE, q_index[0] % SIDE, nu_index[0], site])
    vmem = pl.BlockSpec(memory_space=pltpu.VMEM)
    return pl.pallas_call(
        kernel,
        in_specs=[pl.BlockSpec(memory_space=pltpu.SMEM)] + [vmem] * 4,
        out_specs=[vmem, vmem],
        out_shape=[
            jax.ShapeDtypeStruct((1, W, SITES), jnp.float32),
            jax.ShapeDtypeStruct((1, W), jnp.float32),
        ],
        scratch_shapes=[
            pltpu.VMEM((2 * chips, SITES), jnp.bfloat16),
            pltpu.VMEM((2 * chips, SITES), jnp.bfloat16),
            pltpu.VMEM((LANES, 2 * chips), jnp.float32),
        ],
    )(where.astype(jnp.int32), mine, theirs, jnp.broadcast_to(s, (8, SITES)), source)


def solution(mesh):
    fine = Mesh(mesh.devices.reshape(2, 4, 8, 2, 2), ("xh", "y", "z", "xl", "c"))
    walker, freq = ("xh", "y", "z"), ("xl", "c")
    in_specs = (
        P(walker, None, freq, None),
        P(walker, None, freq, None),
        P(freq),
        P(freq),
        P(freq, walker),
    )
    out_specs = (P(freq, walker, None), P(freq, walker))
    return jax.shard_map(shards, mesh=fine, in_specs=in_specs, out_specs=out_specs, check_vma=False)
```

time: 1030 us -> 107 us (0.10)
  waiting for transfers between devices: 943 us -> 2.93 us
  blocking collectives: 11.5 us -> 78.3 us
  local copies, waits for them, and re-layouts: 46.5 us -> 3.58 us
  Pallas kernels: 0 us -> 14.7 us
  between operations: 15.3 us -> 2.01 us
  matrix products: 10.3 us -> 0 us
    unnamed x6 -> x0, waiting for transfers between devices: 727 us -> none
    all_gather x2 -> x0, waiting for transfers between devices: 215 us -> none  [the longest x1 113 us: shards(): lax.all_gather(up_all, 'walker', axis=0, tiled=True)]
    all_to_all x0 -> x1, blocking collectives: none -> 78.3 us  [shards(): lax.all_to_all(jnp.broadcast_to(block[None], (chips,) + block.shape), CHI...]
    reshape x3 -> x4, local copies, waits for them, and re-layouts: 37.5 us -> 0.25 us  [the longest x2 0.19 us: spread(): block.reshape(SIDE, RUN)]
    pallas_call x0 -> x1, Pallas kernels: none -> 14.7 us  [shards(): pl.pallas_call(kernel, in_specs=[pl.BlockSpec(memory_space=pltpu.SMEM)] +...]
    all_gather x2 -> x0, blocking collectives: 11.5 us -> none  [the longest x1 5.74 us: shards(): lax.all_gather(green_up_blocks, 'freq', axis=2, tiled=True)]
    dot_general x3 -> x0, matrix products: 10.3 us -> none  [the longest x2 9.55 us: term(): jnp.einsum('kn,nkc->cn', current, kernel, precision=lax.Precision.HIGHEST)]
  transfers between devices with their start and end apart: 4 -> 1, of which waited for: 4 -> 1; matrix products, arithmetic and copies ran while one was open for 2% -> 1% of each run, Pallas kernels for 0% -> 0%
where the time goes in v1:
time: 107 us; the launch traced here: 105 us
  blocking collectives  78.3 us (73%)
  Pallas kernels  14.7 us (14%)
  local copies, waits for them, and re-layouts  3.58 us (3%)
  other arithmetic  3.13 us (3%)
  waiting for transfers between devices  2.93 us (3%)
  between operations  2.01 us (2%)
    all_to_all x1, blocking collectives, shards(): lax.all_to_all(jnp.broadcast_to(block[None], (chips,) + block.shape), CHI...  78.3 us
    pallas_call x1, Pallas kernels, shards(): pl.pallas_call(kernel, in_specs=[pl.BlockSpec(memory_space=pltpu.SMEM)] +...  14.7 us
    ppermute x1, waiting for transfers between devices, shards(): theirs = lax.ppermute(mine, 'c', [(0, 1), (1, 0)])  2.93 us
    unnamed x1, local copies, waits for them, and re-layouts  2.18 us
  transfers between devices with their start and end apart: 1, of which 1 were waited for; matrix products, arithmetic and copies ran while one was open for 1% of the time, Pallas kernels for 0%

profile of v1, /device:TPU:2, one launch (start us, length us, event | category | flops | bytes accessed | tf_op | source)
XLA Modules:
  0.0 104.7 jit_solution(16392848199774474971)
XLA Ops:
  0.6 0.7 reduce-precision_convert_fusion.1
  1.3 0.8 reduce
  2.1 0.1 reshape.46
  2.2 0.1 pad_maximum_fusion.1
  2.3 0.8 reduce.1
  3.1 0.1 reshape.48
  3.2 0.3 broadcast_in_dim.4
  3.6 78.3 %all_to_all.5 = bf16[128,80,128]{2,1,0:T(8,128)(2,1)S(1)} all-to-all(bf16[128,80,128]{2,1,0:T(8,128)(2,1)S(1)} %broadcast_in_dim.4), channel_id=1, replica_groups=mesh['xh'=2,'y'=4,'z'=8,'xl'=2,'c'=2] {'xh','y','z','xl'}, dimensions={0} | all-to-all | bytes 5242880 | tf_op jit(solution)/shard_map/all_to_all | solution.py:105
  81.9 2.2 %copy.9 = bf16[16,8,80,128]{3,1,2,0:T(8,128)(2,1)} copy(bf16[16,8,80,128]{3,2,1,0:T(8,128)(2,1)S(1)} %bitcast.15) | data formatting | bytes 5242880
  84.1 0.0 collective-permute-start
  85.4 0.6 pad_add_fusion.where_ref
  86.0 0.1 dynamic-slice_bitcast_fusion
  86.1 0.2 fusion.1
  86.4 0.1 add.43
  86.4 2.9 %collective-permute-done.theirs_ref = bf16[128,10240]{1,0:T(8,128)(2,1)} collective-permute-done((bf16[128,10240]{1,0:T(8,128)(2,1)}, bf16[128,10240]{1,0:T(8,128)(2,1)}, u32[]{:S(2)}, u32[]{:S(2)}) %collective-permute-start) | collective-permute-done | bytes 2621472 | tf_op jit(solution)/shard_map/ppermute | solution.py:115
  89.4 0.6 broadcast_in_dim.5.s_ref
  90.0 14.7 %shard_map.68 = (f32[1,64,4096]{2,1,0:T(8,128)}, f32[1,64]{1,0:T(1,128)}) custom-call(s32[4]{0:T(128)} %pad_add_fusion.where_ref, bf16[128,10240]{1,0:T(8,128)(2,1)} %bitcast.10.mine_ref, bf16[128,10240]{1,0:T(8,128)(2,1)} %collective-permute-done.theirs_ref, f32[8,4096]{1,0:T(8,128)} %broadcast_in_dim.5.s_ref, f32[1,64]{1,0:T(1,128)} %own_ref.1), custom_call_target="tpu_custom_call" | custom-call | tf_op jit(solution)/shard_map/pallas_call | solution.py:119
  (5 shorter events, 0.1 us)
Async XLA Ops:
  84.1 5.3 %collective-permute-start = (bf16[128,10240]{1,0:T(8,128)(2,1)}, bf16[128,10240]{1,0:T(8,128)(2,1)}, u32[]{:S(2)}, u32[]{:S(2)}) collective-permute-start(bf16[128,10240]{1,0:T(8,128)(2,1)} %bitcast.10.mine_ref), channel_id=1, source_target_pairs={{0,1},{1,0},{2,3},{3,2},{4,5},{5,4},{6,7},{7,6},{8,9},{9,8},{10,11... | collective-permute-start | bytes 7864328 | tf_op jit(solution)/shard_map/ppermute | solution.py:115
